TPU v7x, 128 devices: a whole 4x4x4 slice. The times are simulated.
128 devices in a mesh: section: 2 (over z_hi), expert: 8 (over y, z_lo), dp: 8 (over x, core).
Axes of the slice: x: 4, y: 4, z: 4 (z_hi: 2, z_lo: 2; z = z_hi * 2 + z_lo), core: 2. Of those that a mesh axis runs over, the one named last changes fastest.
Arguments:
- inputs: bfloat16 [2, 512, 3072], P(None, ('expert', 'dp')), may hold values from -6 to 6
- cotangent: bfloat16 [2, 512, 3072], P(None, ('expert', 'dp')), may hold values from -6 to 6
- norm_gain: bfloat16 [2, 3072], P('section'), may hold values from 0.5 to 1.5
- router: bfloat16 [2, 3072, 8], P('section'), may hold values from -0.109375 to 0.109375
- w_gate: bfloat16 [2, 8, 3072, 8192], P('section', 'expert', None, 'dp'), may hold values from -0.109375 to 0.109375
- w_up: bfloat16 [2, 8, 3072, 8192], P('section', 'expert', None, 'dp'), may hold values from -0.109375 to 0.109375
- w_down: bfloat16 [2, 8, 8192, 3072], P('section', 'expert', 'dp'), may hold values from -0.0625 to 0.0625
- routes: int32 [2, 2, 512, 2], P('section', None, ('expert', 'dp')), may hold values from 0 to 7, as said below
Outputs:
- acts: bfloat16 [2, 2, 512, 3072], P('section', None, ('expert', 'dp'))
- grads: bfloat16 [2, 2, 512, 3072], P('section', None, ('expert', 'dp'))
- router_grad: float32 [2, 3072, 8], P('section')
Inputs may be any that keep to these rules, and one draw needn't show every extreme that they name: `routes`: the two experts of a token differ. For each layer and micro-batch, the 8 tokens of one device name no expert more than 3 times, and one expert, the same on all devices for that layer and micro-batch, exactly 3 times.
All inputs are finite; a program needn't handle non-finite values.
Results may differ from a plain program's by a relative error of at most 0.017.
Values may be sent and summed in bfloat16 or wider, within the bound.
A program may use at most 128 MiB of HBM per device.

v0:
```python
import jax
import jax.numpy as jnp
from jax import lax
from jax.sharding import PartitionSpec as P

EPSILON = 1e-05


def passed_along(block, axis, distance):
    devices = range(lax.axis_size(axis))
    route = [(i - distance, i) for i in devices if i - distance in devices]
    return lax.ppermute(block, axis, route)


def norm_rows(layer_in, gain_row):
    values = layer_in.astype(jnp.float32)
    inv_rms = lax.rsqrt(jnp.mean(values * values, axis=-1, keepdims=True) + EPSILON)
    return (values, inv_rms, (values * inv_rms * gain_row).astype(jnp.bfloat16))


def gate_probs(hidden, router_w, picks):
    logits = jnp.dot(hidden, router_w, preferred_element_type=jnp.float32)
    chosen = jnp.take_along_axis(logits, picks, axis=1)
    logit_gap = chosen[:, 0] - chosen[:, 1]
    return jnp.stack([jax.nn.sigmoid(logit_gap), jax.nn.sigmoid(-logit_gap)], axis=1)


def slot_table(picks, experts, capacity):
    flat_pick = picks.reshape(-1)
    onehot = (flat_pick[:, None] == jnp.arange(experts, dtype=jnp.int32)[None, :]).astype(jnp.int32)
    earlier = jnp.cumsum(onehot, axis=0) - onehot
    slot_pos = jnp.sum(earlier * onehot, axis=1)
    target = flat_pick * capacity + slot_pos
    return target[:, None] == jnp.arange(experts * capacity, dtype=jnp.int32)[None, :]


def deliver(outgoing, experts, capacity):
    model_width = outgoing.shape[1]
    grouped = outgoing.reshape(experts, capacity, model_width)
    tiled = jnp.repeat(grouped, lax.axis_size("dp"), axis=0)
    arrived = lax.all_to_all(tiled, ("expert", "dp"), split_axis=0, concat_axis=0, tiled=True)
    return arrived.reshape(-1, model_width)


def collect(partial_out, experts, capacity):
    model_width = partial_out.shape[1]
    replicas = lax.axis_size("dp")
    returned = lax.all_to_all(
        partial_out.reshape(experts * replicas, capacity, model_width),
        ("expert", "dp"),
        split_axis=0,
        concat_axis=0,
        tiled=True,
    )
    summed = jnp.sum(
        returned.reshape(experts, replicas, capacity, model_width).astype(jnp.float32), axis=1
    )
    return summed.reshape(experts * capacity, model_width)


def send_rows(placing, row_values):
    grouped = lax.dot_general(
        placing.astype(jnp.bfloat16),
        row_values,
        (((0,), (0,)), ((), ())),
        preferred_element_type=jnp.float32,
    )
    return grouped.astype(jnp.bfloat16)


def forward_layer(layer_in, picks, gain_row, router_w, gate_w, up_w, down_w, experts, capacity):
    values, inv_rms, hidden = norm_rows(layer_in, gain_row)
    gate_prob = gate_probs(hidden, router_w, picks)
    placing = slot_table(picks, experts, capacity)
    arrived = deliver(
        send_rows(placing, jnp.repeat(hidden, picks.shape[1], axis=0)), experts, capacity
    )
    gate_pre = jnp.dot(arrived, gate_w, preferred_element_type=jnp.float32)
    up_pre = jnp.dot(arrived, up_w, preferred_element_type=jnp.float32)
    active = (gate_pre * jax.nn.sigmoid(gate_pre) * up_pre).astype(jnp.bfloat16)
    partial_out = jnp.dot(active, down_w, preferred_element_type=jnp.float32).astype(jnp.bfloat16)
    summed = collect(partial_out, experts, capacity)
    picked = jnp.dot(placing.astype(jnp.float32), summed, precision=lax.Precision.HIGHEST)
    picked = picked.reshape(layer_in.shape[0], picks.shape[1], -1)
    layer_out = (values + jnp.sum(gate_prob[:, :, None] * picked, axis=1)).astype(jnp.bfloat16)
    return (layer_out, picked, gate_pre, up_pre)


def backward_layer(
    layer_in,
    upstream,
    picks,
    gain_row,
    router_w,
    gate_w,
    up_w,
    down_w,
    picked,
    gate_pre,
    up_pre,
    experts,
    capacity,
):
    values, inv_rms, hidden = norm_rows(layer_in, gain_row)
    gate_prob = gate_probs(hidden, router_w, picks)
    placing = slot_table(picks, experts, capacity)
    grad_out = upstream.astype(jnp.float32)
    d_prob = jnp.sum(grad_out[:, None, :] * picked, axis=2)
    d_gap = gate_prob[:, 0] * gate_prob[:, 1] * (d_prob[:, 0] - d_prob[:, 1])
    d_chosen = jnp.stack([d_gap, -d_gap], axis=1)
    expert_hot = (picks[:, :, None] == jnp.arange(experts, dtype=jnp.int32)[None, None, :]).astype(
        jnp.float32
    )
    d_logits = jnp.sum(d_chosen[:, :, None] * expert_hot, axis=1)
    scaled = (gate_prob[:, :, None] * grad_out[:, None, :]).astype(jnp.bfloat16)
    scaled = scaled.reshape(-1, grad_out.shape[1])
    arrived = deliver(send_rows(placing, scaled), experts, capacity)
    contract_last = (((1,), (1,)), ((), ()))
    d_active = lax.dot_general(arrived, down_w, contract_last, preferred_element_type=jnp.float32)
    gate_sig = jax.nn.sigmoid(gate_pre)
    d_gate = (d_active * up_pre * gate_sig * (1.0 + gate_pre * (1.0 - gate_sig))).astype(
        jnp.bfloat16
    )
    d_up = (d_active * gate_pre * gate_sig).astype(jnp.bfloat16)
    d_rows = lax.dot_general(d_gate, gate_w, contract_last, preferred_element_type=jnp.float32)
    d_rows = d_rows + lax.dot_general(d_up, up_w, contract_last, preferred_element_type=jnp.float32)
    summed = collect(d_rows.astype(jnp.bfloat16), experts, capacity)
    returned = jnp.dot(placing.astype(jnp.float32), summed, precision=lax.Precision.HIGHEST)
    returned = returned.reshape(layer_in.shape[0], picks.shape[1], -1)
    d_hidden = jnp.sum(returned, axis=1) + jnp.dot(
        d_logits, router_w.astype(jnp.float32).T, precision=lax.Precision.HIGHEST
    )
    router_term = jnp.dot(hidden.astype(jnp.float32).T, d_logits, precision=lax.Precision.HIGHEST)
    weighted = gain_row * d_hidden
    cubed = inv_rms * inv_rms * inv_rms
    d_in = (
        grad_out
        + inv_rms * weighted
        - values * cubed * jnp.mean(values * weighted, axis=-1, keepdims=True)
    )
    return (d_in.astype(jnp.bfloat16), router_term)


def fetch_micro(stored, which_mb):
    return lax.dynamic_index_in_dim(stored, which_mb, 0, keepdims=False)


def store_micro(stored, fresh, which_mb, in_range):
    previous = lax.dynamic_index_in_dim(stored, which_mb, 0, keepdims=False)
    return lax.dynamic_update_index_in_dim(
        stored, jnp.where(in_range, fresh, previous), which_mb, 0
    )


def per_device(inputs, cotangent, norm_gain, router, w_gate, w_up, w_down, routes):
    section_count = lax.axis_size("section")
    section_id = lax.axis_index("section")
    micro_count, tok_rows, model_width = inputs.shape
    experts = router.shape[2]
    top_k = routes.shape[3]
    capacity = 3 * top_k * tok_rows // (2 * experts)
    gate_w = w_gate[0, 0]
    up_w = w_up[0, 0]
    down_w = w_down[0, 0]
    gain_row = norm_gain[0].astype(jnp.float32)
    router_w = router[0]
    picks_all = routes[0]
    expert_rows = experts * lax.axis_size("dp") * capacity
    hidden_units = gate_w.shape[1]
    tick_count = micro_count + section_count - 1
    carried = jnp.zeros((tok_rows, model_width), jnp.bfloat16)
    outputs_all = jnp.zeros((micro_count, tok_rows, model_width), jnp.bfloat16)
    stash_in = jnp.zeros((micro_count, tok_rows, model_width), jnp.bfloat16)
    stash_pick = jnp.zeros((micro_count, tok_rows, top_k, model_width), jnp.float32)
    stash_gate = jnp.zeros((micro_count, expert_rows, hidden_units), jnp.float32)
    stash_up = jnp.zeros((micro_count, expert_rows, hidden_units), jnp.float32)
    for moment in range(tick_count):
        position = moment - section_id
        in_range = (position >= 0) & (position < micro_count)
        which_mb = jnp.clip(position, 0, micro_count - 1)
        layer_in = jnp.where(section_id == 0, fetch_micro(inputs, which_mb), carried)
        picks = fetch_micro(picks_all, which_mb)
        layer_out, picked, gate_pre, up_pre = forward_layer(
            layer_in, picks, gain_row, router_w, gate_w, up_w, down_w, experts, capacity
        )
        outputs_all = store_micro(outputs_all, layer_out, which_mb, in_range)
        stash_in = store_micro(stash_in, layer_in, which_mb, in_range)
        stash_pick = store_micro(stash_pick, picked, which_mb, in_range)
        stash_gate = store_micro(stash_gate, gate_pre, which_mb, in_range)
        stash_up = store_micro(stash_up, up_pre, which_mb, in_range)
        if moment + 1 < tick_count:
            carried = passed_along(layer_out, "section", 1)
    carried = jnp.zeros((tok_rows, model_width), jnp.bfloat16)
    grads_all = jnp.zeros((micro_count, tok_rows, model_width), jnp.bfloat16)
    router_sum = jnp.zeros((model_width, experts), jnp.float32)
    for moment in range(tick_count):
        position = moment - (section_count - 1 - section_id)
        in_range = (position >= 0) & (position < micro_count)
        which_mb = jnp.clip(position, 0, micro_count - 1)
        upstream = jnp.where(
            section_id == section_count - 1, fetch_micro(cotangent, which_mb), carried
        )
        d_in, router_term = backward_layer(
            fetch_micro(stash_in, which_mb),
            upstream,
            fetch_micro(picks_all, which_mb),
            gain_row,
            router_w,
            gate_w,
            up_w,
            down_w,
            fetch_micro(stash_pick, which_mb),
            fetch_micro(stash_gate, which_mb),
            fetch_micro(stash_up, which_mb),
            experts,
            capacity,
        )
        grads_all = store_micro(grads_all, d_in, which_mb, in_range)
        router_sum = router_sum + jnp.where(in_range, router_term, 0.0)
        if moment + 1 < tick_count:
            carried = passed_along(d_in, "section", -1)
    router_total = lax.psum(router_sum, ("expert", "dp"))
    return (outputs_all[None], grads_all[None], router_total[None])


def solution(mesh):
    placed = (
        P(None, ("expert", "dp"), None),
        P(None, ("expert", "dp"), None),
        P("section", None),
        P("section", None, None),
        P("section", "expert", None, "dp"),
        P("section", "expert", None, "dp"),
        P("section", "expert", "dp", None),
        P("section", None, ("expert", "dp"), None),
    )
    return jax.shard_map(
        per_device,
        mesh=mesh,
        in_specs=placed,
        out_specs=(
            P("section", None, ("expert", "dp"), None),
            P("section", None, ("expert", "dp"), None),
            P("section", None, None),
        ),
        check_vma=False,
    )
```

profile of v0, /device:TPU:0, one launch (start us, length us, event | category | flops | bytes accessed | tf_op | source)
XLA Modules:
  0.0 985.6 jit_solution(17254181758903616295)
XLA Ops:
  13.8 9.5 all-to-all-start
  30.7 16.1 %all-to-all-done = bf16[64,3,3072]{2,1,0:T(4,128)(2,1)S(1)} async-done(((bf16[64,3,3072]{2,1,0:T(4,128)(2,1)}), bf16[64,3,3072]{2,1,0:T(4,128)(2,1)S(1)}, u32[]{:S(2)}, u32[]{:S(2)}) %all-to-all-start) | async-done | bytes 1179680 | tf_op jit(solution)/shard_map/all_to_all | solution.py:41
  61.3 5.1 all-to-all-start.1
  71.7 18.2 %all-to-all-done.1 = bf16[64,3,3072]{2,1,0:T(4,128)(2,1)S(1)} async-done(((bf16[64,3,3072]{2,1,0:T(4,128)(2,1)}), bf16[64,3,3072]{2,1,0:T(4,128)(2,1)S(1)}, u32[]{:S(2)}, u32[]{:S(2)}) %all-to-all-start.1) | async-done | bytes 1179680 | tf_op jit(solution)/shard_map/all_to_all | solution.py:48
  92.8 5.4 collective-permute-start
  104.4 5.7 all-to-all-start.2
  113.1 20.3 %all-to-all-done.2 = bf16[64,3,3072]{2,1,0:T(4,128)(2,1)} async-done(((bf16[64,3,3072]{2,1,0:T(4,128)(2,1)}), bf16[64,3,3072]{2,1,0:T(4,128)(2,1)}, u32[]{:S(2)}, u32[]{:S(2)}) %all-to-all-start.2) | async-done | bytes 1179680 | tf_op jit(solution)/shard_map/all_to_all | solution.py:41
  136.4 5.4 bitcast_dynamic-update-slice_fusion.4
  148.0 5.1 all-to-all-start.3
  155.6 20.9 %all-to-all-done.3 = bf16[64,3,3072]{2,1,0:T(4,128)(2,1)S(1)} async-done(((bf16[64,3,3072]{2,1,0:T(4,128)(2,1)}), bf16[64,3,3072]{2,1,0:T(4,128)(2,1)S(1)}, u32[]{:S(2)}, u32[]{:S(2)}) %all-to-all-start.3) | async-done | bytes 1179680 | tf_op jit(solution)/shard_map/all_to_all | solution.py:48
  189.5 6.0 all-to-all-start.4
  197.9 20.9 %all-to-all-done.4 = bf16[64,3,3072]{2,1,0:T(4,128)(2,1)} async-done(((bf16[64,3,3072]{2,1,0:T(4,128)(2,1)}), bf16[64,3,3072]{2,1,0:T(4,128)(2,1)}, u32[]{:S(2)}, u32[]{:S(2)}) %all-to-all-start.4) | async-done | bytes 1179680 | tf_op jit(solution)/shard_map/all_to_all | solution.py:41
  221.8 5.4 bitcast_dynamic-update-slice_fusion.3
  240.3 21.5 %all-to-all-done.5 = bf16[64,3,3072]{2,1,0:T(4,128)(2,1)S(1)} async-done(((bf16[64,3,3072]{2,1,0:T(4,128)(2,1)}), bf16[64,3,3072]{2,1,0:T(4,128)(2,1)S(1)}, u32[]{:S(2)}, u32[]{:S(2)}) %all-to-all-start.5) | async-done | bytes 1179680 | tf_op jit(solution)/shard_map/all_to_all | solution.py:48
  267.0 5.8 all-to-all-start.6
  275.1 21.1 %all-to-all-done.6 = bf16[64,3,3072]{2,1,0:T(4,128)(2,1)} async-done(((bf16[64,3,3072]{2,1,0:T(4,128)(2,1)}), bf16[64,3,3072]{2,1,0:T(4,128)(2,1)}, u32[]{:S(2)}, u32[]{:S(2)}) %all-to-all-start.6) | async-done | bytes 1179680 | tf_op jit(solution)/shard_map/all_to_all | solution.py:41
  299.0 5.1 fusion.4
  312.3 5.0 all-to-all-start.7
  318.1 22.5 %all-to-all-done.7 = bf16[64,3,3072]{2,1,0:T(4,128)(2,1)S(1)} async-done(((bf16[64,3,3072]{2,1,0:T(4,128)(2,1)}), bf16[64,3,3072]{2,1,0:T(4,128)(2,1)S(1)}, u32[]{:S(2)}, u32[]{:S(2)}) %all-to-all-start.7) | async-done | bytes 1179680 | tf_op jit(solution)/shard_map/all_to_all | solution.py:48
  344.5 5.2 collective-permute-done.2
  352.6 5.8 all-to-all-start.8
  359.3 22.4 %all-to-all-done.8 = bf16[64,3,3072]{2,1,0:T(4,128)(2,1)} async-done(((bf16[64,3,3072]{2,1,0:T(4,128)(2,1)}), bf16[64,3,3072]{2,1,0:T(4,128)(2,1)}, u32[]{:S(2)}, u32[]{:S(2)}) %all-to-all-start.8) | async-done | bytes 1179680 | tf_op jit(solution)/shard_map/all_to_all | solution.py:41
  385.7 5.5 fusion.2
  399.3 4.9 all-to-all-start.9
  405.5 22.2 %all-to-all-done.9 = bf16[64,3,3072]{2,1,0:T(4,128)(2,1)S(1)} async-done(((bf16[64,3,3072]{2,1,0:T(4,128)(2,1)}), bf16[64,3,3072]{2,1,0:T(4,128)(2,1)S(1)}, u32[]{:S(2)}, u32[]{:S(2)}) %all-to-all-start.9) | async-done | bytes 1179680 | tf_op jit(solution)/shard_map/all_to_all | solution.py:48
  430.6 6.2 collective-permute-done.3
  439.6 5.9 all-to-all-start.10
  446.0 22.9 %all-to-all-done.10 = bf16[64,3,3072]{2,1,0:T(4,128)(2,1)} async-done(((bf16[64,3,3072]{2,1,0:T(4,128)(2,1)}), bf16[64,3,3072]{2,1,0:T(4,128)(2,1)}, u32[]{:S(2)}, u32[]{:S(2)}) %all-to-all-start.10) | async-done | bytes 1179680 | tf_op jit(solution)/shard_map/all_to_all | solution.py:41
  472.8 5.5 fusion
  486.4 5.1 all-to-all-start.11
  493.0 21.9 %all-to-all-done.11 = bf16[64,3,3072]{2,1,0:T(4,128)(2,1)S(1)} async-done(((bf16[64,3,3072]{2,1,0:T(4,128)(2,1)}), bf16[64,3,3072]{2,1,0:T(4,128)(2,1)S(1)}, u32[]{:S(2)}, u32[]{:S(2)}) %all-to-all-start.11) | async-done | bytes 1179680 | tf_op jit(solution)/shard_map/all_to_all | solution.py:48
  516.5 460.3 %all-reduce.2.cloned.1.call-done = f32[1,3072,8]{1,2,0:T(8,128)} async-done(((f32[1,3072,8]{1,2,0:T(8,128)}), f32[1,3072,8]{1,2,0:T(8,128)}) %all-reduce.2.cloned.1.call-update) | async-done | bytes 98320 | tf_op jit(solution)/shard_map/psum | solution.py:222
  (484 shorter events, 150.3 us)
Async XLA Ops:
  13.8 33.0 %all-to-all-start = ((bf16[64,3,3072]{2,1,0:T(4,128)(2,1)}), bf16[64,3,3072]{2,1,0:T(4,128)(2,1)S(1)}, u32[]{:S(2)}, u32[]{:S(2)}) async-start(bf16[64,3,3072]{2,1,0:T(4,128)(2,1)} %bitcast.7), calls=%async_computation | async-start | bytes 3145728 | tf_op jit(solution)/shard_map/all_to_all | solution.py:41
  30.7 36.4 %copy-start.24 = (f32[8,3072]{1,0:T(8,128)}, f32[8,3072]{1,0:T(8,128)S(1)}, u32[]{:S(2)}) copy-start(f32[8,3072]{1,0:T(8,128)S(1)} %bitcast_convert_fusion) | copy-start | bytes 294916
  57.0 41.2 %copy-start.1 = (f32[2,192,1024]{2,1,0:T(8,128)}, f32[2,192,1024]{2,1,0:T(8,128)S(1)}, u32[]{:S(2)}) copy-start(f32[2,192,1024]{2,1,0:T(8,128)S(1)} %get-tuple-element.57) | copy-start | bytes 4718596
  61.3 28.5 %all-to-all-start.1 = ((bf16[64,3,3072]{2,1,0:T(4,128)(2,1)}), bf16[64,3,3072]{2,1,0:T(4,128)(2,1)S(1)}, u32[]{:S(2)}, u32[]{:S(2)}) async-start(bf16[64,3,3072]{2,1,0:T(4,128)(2,1)} %reshape.574), calls=%async_computation.1 | async-start | bytes 3145728 | tf_op jit(solution)/shard_map/all_to_all | solution.py:48
  69.6 22.8 %copy-start.54 = (s32[8,2]{0,1:T(2,128)S(1)}, s32[8,2]{0,1:T(2,128)}, u32[]{:S(2)}) copy-start(s32[8,2]{0,1:T(2,128)} %multiply_add_fusion.5) | copy-start | bytes 196
  92.8 8.0 collective-permute-start
  104.4 29.0 %all-to-all-start.2 = ((bf16[64,3,3072]{2,1,0:T(4,128)(2,1)}), bf16[64,3,3072]{2,1,0:T(4,128)(2,1)}, u32[]{:S(2)}, u32[]{:S(2)}) async-start(bf16[64,3,3072]{2,1,0:T(4,128)(2,1)} %bitcast.17), calls=%async_computation.2 | async-start | bytes 3145728 | tf_op jit(solution)/shard_map/all_to_all | solution.py:41
  148.0 28.5 %all-to-all-start.3 = ((bf16[64,3,3072]{2,1,0:T(4,128)(2,1)}), bf16[64,3,3072]{2,1,0:T(4,128)(2,1)S(1)}, u32[]{:S(2)}, u32[]{:S(2)}) async-start(bf16[64,3,3072]{2,1,0:T(4,128)(2,1)} %reshape.580), calls=%async_computation.3 | async-start | bytes 3145728 | tf_op jit(solution)/shard_map/all_to_all | solution.py:48
  155.6 23.6 %copy-start.53 = (s32[8,2]{0,1:T(2,128)S(1)}, s32[8,2]{0,1:T(2,128)}, u32[]{:S(2)}) copy-start(s32[8,2]{0,1:T(2,128)} %multiply_add_fusion.4) | copy-start | bytes 196
  155.6 29.7 %copy-start.4 = (f32[2,192,1024]{2,1,0:T(8,128)S(1)}, f32[2,192,1024]{2,1,0:T(8,128)}, u32[]{:S(2)}) copy-start(f32[2,192,1024]{2,1,0:T(8,128)} %copy-done.3) | copy-start | bytes 4718596
  180.3 6.7 collective-permute-start.1
  189.5 29.4 %all-to-all-start.4 = ((bf16[64,3,3072]{2,1,0:T(4,128)(2,1)}), bf16[64,3,3072]{2,1,0:T(4,128)(2,1)}, u32[]{:S(2)}, u32[]{:S(2)}) async-start(bf16[64,3,3072]{2,1,0:T(4,128)(2,1)} %bitcast.26), calls=%async_computation.4 | async-start | bytes 3145728 | tf_op jit(solution)/shard_map/all_to_all | solution.py:41
  233.4 28.4 %all-to-all-start.5 = ((bf16[64,3,3072]{2,1,0:T(4,128)(2,1)}), bf16[64,3,3072]{2,1,0:T(4,128)(2,1)S(1)}, u32[]{:S(2)}, u32[]{:S(2)}) async-start(bf16[64,3,3072]{2,1,0:T(4,128)(2,1)} %reshape.586), calls=%async_computation.5 | async-start | bytes 3145728 | tf_op jit(solution)/shard_map/all_to_all | solution.py:48
  240.3 22.7 %copy-start.18 = (f32[2,8,2,3072]{3,1,2,0:T(8,128)S(1)}, f32[2,8,2,3072]{3,1,2,0:T(8,128)}, u32[]{:S(2)}) copy-start(f32[2,8,2,3072]{3,1,2,0:T(8,128)} %copy-done.17) | copy-start | bytes 1179652
  240.3 22.7 %copy-start.35 = (f32[1,8,2,3072]{3,1,2,0:T(8,128)S(1)}, f32[1,8,2,3072]{3,1,2,0:T(8,128)}, u32[]{:S(2)}) copy-start(f32[1,8,2,3072]{3,1,2,0:T(8,128)} %constant_dynamic-slice_fusion.6) | copy-start | bytes 589828
  267.0 37.1 %slice-start = ((s8[6291456]{0:T(1024)(128)(4,1)}), s8[2097152]{0:T(1024)(128)(4,1)S(1)}, s32[]{:S(2)}) async-start(s8[6291456]{0:T(1024)(128)(4,1)} %bitcast.549), calls=%async_computation.13 | async-start | bytes 4194304
  267.0 29.1 %all-to-all-start.6 = ((bf16[64,3,3072]{2,1,0:T(4,128)(2,1)}), bf16[64,3,3072]{2,1,0:T(4,128)(2,1)}, u32[]{:S(2)}, u32[]{:S(2)}) async-start(bf16[64,3,3072]{2,1,0:T(4,128)(2,1)} %bitcast.569), calls=%async_computation.6 | async-start | bytes 3145728 | tf_op jit(solution)/shard_map/all_to_all | solution.py:41
  312.3 28.4 %all-to-all-start.7 = ((bf16[64,3,3072]{2,1,0:T(4,128)(2,1)}), bf16[64,3,3072]{2,1,0:T(4,128)(2,1)S(1)}, u32[]{:S(2)}, u32[]{:S(2)}) async-start(bf16[64,3,3072]{2,1,0:T(4,128)(2,1)} %reshape.592), calls=%async_computation.7 | async-start | bytes 3145728 | tf_op jit(solution)/shard_map/all_to_all | solution.py:48
  318.1 24.0 %copy-start.39 = (bf16[2,8,3072]{2,1,0:T(8,128)(2,1)S(1)}, bf16[2,8,3072]{2,1,0:T(8,128)(2,1)}, u32[]{:S(2)}) copy-start(bf16[2,8,3072]{2,1,0:T(8,128)(2,1)} %param.11) | copy-start | bytes 294916
  318.1 24.0 %copy-start.59 = (f32[8]{0:T(128)S(1)}, f32[8]{0:T(128)}, u32[]{:S(2)}) copy-start(f32[8]{0:T(128)} %copy-done.58) | copy-start | bytes 100
  318.1 24.0 %copy-start.70 = (f32[8]{0:T(128)S(1)}, f32[8]{0:T(128)}, u32[]{:S(2)}) copy-start(f32[8]{0:T(128)} %get-tuple-element.49) | copy-start | bytes 100
  342.3 7.5 collective-permute-start.2
  352.6 38.6 %slice-start.2 = ((s8[6291456]{0:T(1024)(128)(4,1)}), s8[2097152]{0:T(1024)(128)(4,1)S(1)}, s32[]{:S(2)}) async-start(s8[6291456]{0:T(1024)(128)(4,1)} %bitcast.551), calls=%async_computation.15 | async-start | bytes 4194304
  352.6 29.2 %all-to-all-start.8 = ((bf16[64,3,3072]{2,1,0:T(4,128)(2,1)}), bf16[64,3,3072]{2,1,0:T(4,128)(2,1)}, u32[]{:S(2)}, u32[]{:S(2)}) async-start(bf16[64,3,3072]{2,1,0:T(4,128)(2,1)} %bitcast.567), calls=%async_computation.8 | async-start | bytes 3145728 | tf_op jit(solution)/shard_map/all_to_all | solution.py:41
  399.3 28.4 %all-to-all-start.9 = ((bf16[64,3,3072]{2,1,0:T(4,128)(2,1)}), bf16[64,3,3072]{2,1,0:T(4,128)(2,1)S(1)}, u32[]{:S(2)}, u32[]{:S(2)}) async-start(bf16[64,3,3072]{2,1,0:T(4,128)(2,1)} %reshape.598), calls=%async_computation.9 | async-start | bytes 3145728 | tf_op jit(solution)/shard_map/all_to_all | solution.py:48
  429.3 7.5 collective-permute-start.3
  439.6 38.7 %slice-start.4 = ((s8[6291456]{0:T(1024)(128)(4,1)}), s8[2097152]{0:T(1024)(128)(4,1)S(1)}, s32[]{:S(2)}) async-start(s8[6291456]{0:T(1024)(128)(4,1)} %bitcast.553), calls=%async_computation.17 | async-start | bytes 4194304
  439.6 29.2 %all-to-all-start.10 = ((bf16[64,3,3072]{2,1,0:T(4,128)(2,1)}), bf16[64,3,3072]{2,1,0:T(4,128)(2,1)}, u32[]{:S(2)}, u32[]{:S(2)}) async-start(bf16[64,3,3072]{2,1,0:T(4,128)(2,1)} %bitcast.568), calls=%async_computation.10 | async-start | bytes 3145728 | tf_op jit(solution)/shard_map/all_to_all | solution.py:41
  486.4 28.5 %all-to-all-start.11 = ((bf16[64,3,3072]{2,1,0:T(4,128)(2,1)}), bf16[64,3,3072]{2,1,0:T(4,128)(2,1)S(1)}, u32[]{:S(2)}, u32[]{:S(2)}) async-start(bf16[64,3,3072]{2,1,0:T(4,128)(2,1)} %reshape.604), calls=%async_computation.11 | async-start | bytes 3145728 | tf_op jit(solution)/shard_map/all_to_all | solution.py:48
  491.5 485.3 %all-reduce.2.cloned.1.call-start = ((), (), s32[]{:S(2)}) async-start(), calls=%async_computation.12 | async-start | bytes 196608 | tf_op jit(solution)/shard_map/psum | solution.py:222
  491.6 24.2 %copy-start.43 = (bf16[1,2,8,3072]{3,2,1,0:T(8,128)(2,1)}, bf16[1,2,8,3072]{3,2,1,0:T(8,128)(2,1)S(1)}, u32[]{:S(2)}) copy-start(bf16[1,2,8,3072]{3,2,1,0:T(8,128)(2,1)S(1)} %fusion.176) | copy-start | bytes 294916
  516.5 461.8 %copy-start.42 = (bf16[1,2,8,3072]{3,2,1,0:T(8,128)(2,1)}, bf16[1,2,8,3072]{3,2,1,0:T(8,128)(2,1)S(1)}, u32[]{:S(2)}) copy-start(bf16[1,2,8,3072]{3,2,1,0:T(8,128)(2,1)S(1)} %fusion.188) | copy-start | bytes 294916
  (80 other events, 451.5 us)
Sparse Core Ops, SparseCore 0:
  495.3 481.3 all-reduce.1
where the time goes:
time: 996 us; the launch traced here: 986 us
  waiting for transfers between devices  723 us (73%)
  starting transfers between devices  81.9 us (8%)
  local copies, waits for them, and re-layouts  79.4 us (8%)
  matrix products  65.2 us (7%)
  other arithmetic  19.5 us (2%)
  between operations  16.4 us (2%)
    psum x1, waiting for transfers between devices, per_device(): router_total = lax.psum(router_sum, ('expert', 'dp'))  460 us
    all_to_all x6, waiting for transfers between devices, collect(): lax.all_to_all(partial_out.reshape(experts * replicas, capacity, model_wi...  127 us
    all_to_all x6, waiting for transfers between devices, deliver(): lax.all_to_all(tiled, ('expert', 'dp'), split_axis=0, concat_axis=0, tile...  124 us
    all_to_all x6, starting transfers between devices, deliver(): lax.all_to_all(tiled, ('expert', 'dp'), split_axis=0, concat_axis=0, tile...  38.8 us
    all_to_all x6, starting transfers between devices, collect(): lax.all_to_all(partial_out.reshape(experts * replicas, capacity, model_wi...  30.1 us
  transfers between devices with their start and end apart: 17, of which 16 were waited for; matrix products, arithmetic and copies ran while one was open for 3% of the time, Pallas kernels for 0%

commit v1 on v0

--- a/solution.py
+++ b/solution.py
@@ -219,7 +219,7 @@
         router_sum = router_sum + jnp.where(in_range, router_term, 0.0)
         if moment + 1 < tick_count:
             carried = passed_along(d_in, "section", -1)
-    router_total = lax.psum(router_sum, ("expert", "dp"))
+    router_total = lax.psum(lax.psum(router_sum, "expert"), "dp")
     return (outputs_all[None], grads_all[None], router_total[None])
 
 

time: 996 us -> 649 us (0.65)
  waiting for transfers between devices: 723 us -> 376 us
    psum x1 -> x2, waiting for transfers between devices: 460 us -> 135 us  [per_device(): router_total = lax.psum(lax.psum(router_sum, 'expert'), 'dp')]
    all_to_all x6, waiting for transfers between devices: 127 us -> 105 us  [collect(): lax.all_to_all(partial_out.reshape(experts * replicas, capacity, model_wi...]
  transfers between devices with their start and end apart: 17 -> 18, of which waited for: 16 -> 16; matrix products, arithmetic and copies ran while one was open for 3% -> 5% of each run, Pallas kernels for 0% -> 0%
where the time goes in v1:
time: 649 us; the launch traced here: 638 us
  waiting for transfers between devices  376 us (58%)
  starting transfers between devices  81.9 us (13%)
  local copies, waits for them, and re-layouts  79.4 us (12%)
  matrix products  65.2 us (10%)
  other arithmetic  19.5 us (3%)
  between operations  16.4 us (3%)
    psum x2, waiting for transfers between devices, per_device(): router_total = lax.psum(lax.psum(router_sum, 'expert'), 'dp')  135 us
    all_to_all x6, waiting for transfers between devices, deliver(): lax.all_to_all(tiled, ('expert', 'dp'), split_axis=0, concat_axis=0, tile...  124 us
    all_to_all x6, waiting for transfers between devices, collect(): lax.all_to_all(partial_out.reshape(experts * replicas, capacity, model_wi...  105 us
    all_to_all x6, starting transfers between devices, deliver(): lax.all_to_all(tiled, ('expert', 'dp'), split_axis=0, concat_axis=0, tile...  38.8 us
    all_to_all x6, starting transfers between devices, collect(): lax.all_to_all(partial_out.reshape(experts * replicas, capacity, model_wi...  30.1 us
    reshape x6, local copies, waits for them, and re-layouts, deliver(): return arrived.reshape(-1, model_width)  17.6 us
    dot_general x3, matrix products, backward_layer(): lax.dot_general(arrived, down_w, contract_last, preferred_element_type=jn...  16.2 us
    dot_general x3, matrix products, forward_layer(): up_pre = jnp.dot(arrived, up_w, preferred_element_type=jnp.float32)  15.6 us
  transfers between devices with their start and end apart: 18, of which 16 were waited for; matrix products, arithmetic and copies ran while one was open for 5% of the time, Pallas kernels for 0%

profile of v1, /device:TPU:0, one launch (start us, length us, event | category | flops | bytes accessed | tf_op | source)
XLA Modules:
  0.0 638.5 jit_solution(10092944083179647833)
XLA Ops:
  13.8 9.5 %all-to-all-start = ((bf16[64,3,3072]{2,1,0:T(4,128)(2,1)}), bf16[64,3,3072]{2,1,0:T(4,128)(2,1)S(1)}, u32[]{:S(2)}, u32[]{:S(2)}) async-start(bf16[64,3,3072]{2,1,0:T(4,128)(2,1)} %bitcast.7), calls=%async_computation | async-start | bytes 3145728 | tf_op jit(solution)/shard_map/all_to_all | solution.py:41
  30.7 16.1 %all-to-all-done = bf16[64,3,3072]{2,1,0:T(4,128)(2,1)S(1)} async-done(((bf16[64,3,3072]{2,1,0:T(4,128)(2,1)}), bf16[64,3,3072]{2,1,0:T(4,128)(2,1)S(1)}, u32[]{:S(2)}, u32[]{:S(2)}) %all-to-all-start) | async-done | bytes 1179680 | tf_op jit(solution)/shard_map/all_to_all | solution.py:41
  61.3 5.1 all-to-all-start.1
  71.7 18.2 %all-to-all-done.1 = bf16[64,3,3072]{2,1,0:T(4,128)(2,1)S(1)} async-done(((bf16[64,3,3072]{2,1,0:T(4,128)(2,1)}), bf16[64,3,3072]{2,1,0:T(4,128)(2,1)S(1)}, u32[]{:S(2)}, u32[]{:S(2)}) %all-to-all-start.1) | async-done | bytes 1179680 | tf_op jit(solution)/shard_map/all_to_all | solution.py:48
  92.8 5.4 collective-permute-start
  104.4 5.7 all-to-all-start.2
  113.1 20.3 %all-to-all-done.2 = bf16[64,3,3072]{2,1,0:T(4,128)(2,1)} async-done(((bf16[64,3,3072]{2,1,0:T(4,128)(2,1)}), bf16[64,3,3072]{2,1,0:T(4,128)(2,1)}, u32[]{:S(2)}, u32[]{:S(2)}) %all-to-all-start.2) | async-done | bytes 1179680 | tf_op jit(solution)/shard_map/all_to_all | solution.py:41
  136.4 5.4 bitcast_dynamic-update-slice_fusion.4
  148.0 5.1 all-to-all-start.3
  155.6 20.9 %all-to-all-done.3 = bf16[64,3,3072]{2,1,0:T(4,128)(2,1)S(1)} async-done(((bf16[64,3,3072]{2,1,0:T(4,128)(2,1)}), bf16[64,3,3072]{2,1,0:T(4,128)(2,1)S(1)}, u32[]{:S(2)}, u32[]{:S(2)}) %all-to-all-start.3) | async-done | bytes 1179680 | tf_op jit(solution)/shard_map/all_to_all | solution.py:48
  189.5 6.0 all-to-all-start.4
  197.9 20.9 %all-to-all-done.4 = bf16[64,3,3072]{2,1,0:T(4,128)(2,1)} async-done(((bf16[64,3,3072]{2,1,0:T(4,128)(2,1)}), bf16[64,3,3072]{2,1,0:T(4,128)(2,1)}, u32[]{:S(2)}, u32[]{:S(2)}) %all-to-all-start.4) | async-done | bytes 1179680 | tf_op jit(solution)/shard_map/all_to_all | solution.py:41
  221.8 5.4 bitcast_dynamic-update-slice_fusion.3
  240.3 21.5 %all-to-all-done.5 = bf16[64,3,3072]{2,1,0:T(4,128)(2,1)S(1)} async-done(((bf16[64,3,3072]{2,1,0:T(4,128)(2,1)}), bf16[64,3,3072]{2,1,0:T(4,128)(2,1)S(1)}, u32[]{:S(2)}, u32[]{:S(2)}) %all-to-all-start.5) | async-done | bytes 1179680 | tf_op jit(solution)/shard_map/all_to_all | solution.py:48
  267.0 5.8 all-to-all-start.6
  275.1 21.1 %all-to-all-done.6 = bf16[64,3,3072]{2,1,0:T(4,128)(2,1)} async-done(((bf16[64,3,3072]{2,1,0:T(4,128)(2,1)}), bf16[64,3,3072]{2,1,0:T(4,128)(2,1)}, u32[]{:S(2)}, u32[]{:S(2)}) %all-to-all-start.6) | async-done | bytes 1179680 | tf_op jit(solution)/shard_map/all_to_all | solution.py:41
  299.0 5.1 fusion.4
  312.3 5.0 all-to-all-start.7
  318.1 22.5 %all-to-all-done.7 = bf16[64,3,3072]{2,1,0:T(4,128)(2,1)S(1)} async-done(((bf16[64,3,3072]{2,1,0:T(4,128)(2,1)}), bf16[64,3,3072]{2,1,0:T(4,128)(2,1)S(1)}, u32[]{:S(2)}, u32[]{:S(2)}) %all-to-all-start.7) | async-done | bytes 1179680 | tf_op jit(solution)/shard_map/all_to_all | solution.py:48
  344.5 5.2 collective-permute-done.2
  352.6 5.8 all-to-all-start.8
  359.3 22.4 %all-to-all-done.8 = bf16[64,3,3072]{2,1,0:T(4,128)(2,1)} async-done(((bf16[64,3,3072]{2,1,0:T(4,128)(2,1)}), bf16[64,3,3072]{2,1,0:T(4,128)(2,1)}, u32[]{:S(2)}, u32[]{:S(2)}) %all-to-all-start.8) | async-done | bytes 1179680 | tf_op jit(solution)/shard_map/all_to_all | solution.py:41
  385.7 5.5 fusion.2
  399.3 4.9 all-to-all-start.9
  405.5 22.2 %all-to-all-done.9 = bf16[64,3,3072]{2,1,0:T(4,128)(2,1)S(1)} async-done(((bf16[64,3,3072]{2,1,0:T(4,128)(2,1)}), bf16[64,3,3072]{2,1,0:T(4,128)(2,1)S(1)}, u32[]{:S(2)}, u32[]{:S(2)}) %all-to-all-start.9) | async-done | bytes 1179680 | tf_op jit(solution)/shard_map/all_to_all | solution.py:48
  430.6 6.2 collective-permute-done.3
  439.6 5.9 all-to-all-start.10
  446.0 22.9 %all-to-all-done.10 = bf16[64,3,3072]{2,1,0:T(4,128)(2,1)} async-done(((bf16[64,3,3072]{2,1,0:T(4,128)(2,1)}), bf16[64,3,3072]{2,1,0:T(4,128)(2,1)}, u32[]{:S(2)}, u32[]{:S(2)}) %all-to-all-start.10) | async-done | bytes 1179680 | tf_op jit(solution)/shard_map/all_to_all | solution.py:41
  472.8 5.5 fusion
  486.4 5.1 all-to-all-start.11
  493.1 77.0 %all-reduce.3.cloned.1.call-done = f32[3072,8]{0,1:T(8,128)} async-done(((f32[3072,8]{0,1:T(8,128)}), f32[3072,8]{0,1:T(8,128)}) %all-reduce.3.cloned.1.call-update) | async-done | bytes 98320 | tf_op jit(solution)/shard_map/psum | solution.py:222
  571.7 58.0 %all-reduce.5.cloned.1.call-done = f32[1,3072,8]{1,2,0:T(8,128)} async-done(((f32[1,3072,8]{1,2,0:T(8,128)}), f32[1,3072,8]{1,2,0:T(8,128)}) %all-reduce.5.cloned.1.call-update) | async-done | bytes 98320 | tf_op jit(solution)/shard_map/psum | solution.py:222
  (487 shorter events, 150.4 us)
Async XLA Ops:
  13.8 33.0 %all-to-all-start = ((bf16[64,3,3072]{2,1,0:T(4,128)(2,1)}), bf16[64,3,3072]{2,1,0:T(4,128)(2,1)S(1)}, u32[]{:S(2)}, u32[]{:S(2)}) async-start(bf16[64,3,3072]{2,1,0:T(4,128)(2,1)} %bitcast.7), calls=%async_computation | async-start | bytes 3145728 | tf_op jit(solution)/shard_map/all_to_all | solution.py:41
  30.7 36.4 %copy-start.24 = (f32[8,3072]{1,0:T(8,128)}, f32[8,3072]{1,0:T(8,128)S(1)}, u32[]{:S(2)}) copy-start(f32[8,3072]{1,0:T(8,128)S(1)} %bitcast_convert_fusion) | copy-start | bytes 294916
  57.0 41.2 %copy-start.1 = (f32[2,192,1024]{2,1,0:T(8,128)}, f32[2,192,1024]{2,1,0:T(8,128)S(1)}, u32[]{:S(2)}) copy-start(f32[2,192,1024]{2,1,0:T(8,128)S(1)} %get-tuple-element.57) | copy-start | bytes 4718596
  61.3 28.5 %all-to-all-start.1 = ((bf16[64,3,3072]{2,1,0:T(4,128)(2,1)}), bf16[64,3,3072]{2,1,0:T(4,128)(2,1)S(1)}, u32[]{:S(2)}, u32[]{:S(2)}) async-start(bf16[64,3,3072]{2,1,0:T(4,128)(2,1)} %reshape.574), calls=%async_computation.1 | async-start | bytes 3145728 | tf_op jit(solution)/shard_map/all_to_all | solution.py:48
  69.6 22.8 %copy-start.54 = (s32[8,2]{0,1:T(2,128)S(1)}, s32[8,2]{0,1:T(2,128)}, u32[]{:S(2)}) copy-start(s32[8,2]{0,1:T(2,128)} %multiply_add_fusion.5) | copy-start | bytes 196
  92.8 8.0 %collective-permute-start = (bf16[8,3072]{1,0:T(8,128)(2,1)S(1)}, bf16[8,3072]{1,0:T(8,128)(2,1)S(1)}, u32[]{:S(2)}, u32[]{:S(2)}) collective-permute-start(bf16[8,3072]{1,0:T(8,128)(2,1)S(1)} %fusion.158), channel_id=1, source_target_pairs={{0,64},{1,65},{2,66},{3,67},{4,68},{5,69},{6,70},{7,71},{8,72},{9,... | collective-permute-start | bytes 147464 | tf_op jit(solution)/shard_map/ppermute | solution.py:12
  104.4 29.0 %all-to-all-start.2 = ((bf16[64,3,3072]{2,1,0:T(4,128)(2,1)}), bf16[64,3,3072]{2,1,0:T(4,128)(2,1)}, u32[]{:S(2)}, u32[]{:S(2)}) async-start(bf16[64,3,3072]{2,1,0:T(4,128)(2,1)} %bitcast.17), calls=%async_computation.2 | async-start | bytes 3145728 | tf_op jit(solution)/shard_map/all_to_all | solution.py:41
  148.0 28.5 %all-to-all-start.3 = ((bf16[64,3,3072]{2,1,0:T(4,128)(2,1)}), bf16[64,3,3072]{2,1,0:T(4,128)(2,1)S(1)}, u32[]{:S(2)}, u32[]{:S(2)}) async-start(bf16[64,3,3072]{2,1,0:T(4,128)(2,1)} %reshape.580), calls=%async_computation.3 | async-start | bytes 3145728 | tf_op jit(solution)/shard_map/all_to_all | solution.py:48
  155.6 23.6 %copy-start.53 = (s32[8,2]{0,1:T(2,128)S(1)}, s32[8,2]{0,1:T(2,128)}, u32[]{:S(2)}) copy-start(s32[8,2]{0,1:T(2,128)} %multiply_add_fusion.4) | copy-start | bytes 196
  155.6 29.7 %copy-start.4 = (f32[2,192,1024]{2,1,0:T(8,128)S(1)}, f32[2,192,1024]{2,1,0:T(8,128)}, u32[]{:S(2)}) copy-start(f32[2,192,1024]{2,1,0:T(8,128)} %copy-done.3) | copy-start | bytes 4718596
  180.3 6.7 %collective-permute-start.1 = (bf16[8,3072]{1,0:T(8,128)(2,1)S(1)}, bf16[8,3072]{1,0:T(8,128)(2,1)S(1)}, u32[]{:S(2)}, u32[]{:S(2)}) collective-permute-start(bf16[8,3072]{1,0:T(8,128)(2,1)S(1)} %get-tuple-element.28), channel_id=1, source_target_pairs={{0,64},{1,65},{2,66},{3,67},{4,68},{5,69},{6,70},{7,71},{8,72},{9,... | collective-permute-start | bytes 147464 | tf_op jit(solution)/shard_map/ppermute | solution.py:12
  189.5 29.4 %all-to-all-start.4 = ((bf16[64,3,3072]{2,1,0:T(4,128)(2,1)}), bf16[64,3,3072]{2,1,0:T(4,128)(2,1)}, u32[]{:S(2)}, u32[]{:S(2)}) async-start(bf16[64,3,3072]{2,1,0:T(4,128)(2,1)} %bitcast.26), calls=%async_computation.4 | async-start | bytes 3145728 | tf_op jit(solution)/shard_map/all_to_all | solution.py:41
  233.4 28.4 %all-to-all-start.5 = ((bf16[64,3,3072]{2,1,0:T(4,128)(2,1)}), bf16[64,3,3072]{2,1,0:T(4,128)(2,1)S(1)}, u32[]{:S(2)}, u32[]{:S(2)}) async-start(bf16[64,3,3072]{2,1,0:T(4,128)(2,1)} %reshape.586), calls=%async_computation.5 | async-start | bytes 3145728 | tf_op jit(solution)/shard_map/all_to_all | solution.py:48
  240.3 22.7 %copy-start.18 = (f32[2,8,2,3072]{3,1,2,0:T(8,128)S(1)}, f32[2,8,2,3072]{3,1,2,0:T(8,128)}, u32[]{:S(2)}) copy-start(f32[2,8,2,3072]{3,1,2,0:T(8,128)} %copy-done.17) | copy-start | bytes 1179652
  267.0 37.1 %slice-start = ((s8[6291456]{0:T(1024)(128)(4,1)}), s8[2097152]{0:T(1024)(128)(4,1)S(1)}, s32[]{:S(2)}) async-start(s8[6291456]{0:T(1024)(128)(4,1)} %bitcast.548), calls=%async_computation.14 | async-start | bytes 4194304
  267.0 29.1 %all-to-all-start.6 = ((bf16[64,3,3072]{2,1,0:T(4,128)(2,1)}), bf16[64,3,3072]{2,1,0:T(4,128)(2,1)}, u32[]{:S(2)}, u32[]{:S(2)}) async-start(bf16[64,3,3072]{2,1,0:T(4,128)(2,1)} %bitcast.568), calls=%async_computation.6 | async-start | bytes 3145728 | tf_op jit(solution)/shard_map/all_to_all | solution.py:41
  312.3 28.4 %all-to-all-start.7 = ((bf16[64,3,3072]{2,1,0:T(4,128)(2,1)}), bf16[64,3,3072]{2,1,0:T(4,128)(2,1)S(1)}, u32[]{:S(2)}, u32[]{:S(2)}) async-start(bf16[64,3,3072]{2,1,0:T(4,128)(2,1)} %reshape.592), calls=%async_computation.7 | async-start | bytes 3145728 | tf_op jit(solution)/shard_map/all_to_all | solution.py:48
  318.1 24.0 %copy-start.39 = (bf16[2,8,3072]{2,1,0:T(8,128)(2,1)S(1)}, bf16[2,8,3072]{2,1,0:T(8,128)(2,1)}, u32[]{:S(2)}) copy-start(bf16[2,8,3072]{2,1,0:T(8,128)(2,1)} %param.11) | copy-start | bytes 294916
  318.1 24.0 %copy-start.59 = (f32[8]{0:T(128)S(1)}, f32[8]{0:T(128)}, u32[]{:S(2)}) copy-start(f32[8]{0:T(128)} %copy-done.58) | copy-start | bytes 100
  318.1 24.0 %copy-start.70 = (f32[8]{0:T(128)S(1)}, f32[8]{0:T(128)}, u32[]{:S(2)}) copy-start(f32[8]{0:T(128)} %get-tuple-element.49) | copy-start | bytes 100
  342.3 7.5 %collective-permute-start.2 = (bf16[8,3072]{1,0:T(8,128)(2,1)S(1)}, bf16[8,3072]{1,0:T(8,128)(2,1)S(1)}, u32[]{:S(2)}, u32[]{:S(2)}) collective-permute-start(bf16[8,3072]{1,0:T(8,128)(2,1)S(1)} %get-tuple-element.18), channel_id=1, source_target_pairs={{64,0},{65,1},{66,2},{67,3},{68,4},{69,5},{70,6},{71,7},{72,8},{73... | collective-permute-start | bytes 147464 | tf_op jit(solution)/shard_map/ppermute | solution.py:12
  352.6 38.6 %slice-start.2 = ((s8[6291456]{0:T(1024)(128)(4,1)}), s8[2097152]{0:T(1024)(128)(4,1)S(1)}, s32[]{:S(2)}) async-start(s8[6291456]{0:T(1024)(128)(4,1)} %bitcast.550), calls=%async_computation.16 | async-start | bytes 4194304
  352.6 29.2 %all-to-all-start.8 = ((bf16[64,3,3072]{2,1,0:T(4,128)(2,1)}), bf16[64,3,3072]{2,1,0:T(4,128)(2,1)}, u32[]{:S(2)}, u32[]{:S(2)}) async-start(bf16[64,3,3072]{2,1,0:T(4,128)(2,1)} %bitcast.566), calls=%async_computation.8 | async-start | bytes 3145728 | tf_op jit(solution)/shard_map/all_to_all | solution.py:41
  399.3 28.4 %all-to-all-start.9 = ((bf16[64,3,3072]{2,1,0:T(4,128)(2,1)}), bf16[64,3,3072]{2,1,0:T(4,128)(2,1)S(1)}, u32[]{:S(2)}, u32[]{:S(2)}) async-start(bf16[64,3,3072]{2,1,0:T(4,128)(2,1)} %reshape.598), calls=%async_computation.9 | async-start | bytes 3145728 | tf_op jit(solution)/shard_map/all_to_all | solution.py:48
  429.3 7.5 %collective-permute-start.3 = (bf16[8,3072]{1,0:T(8,128)(2,1)S(1)}, bf16[8,3072]{1,0:T(8,128)(2,1)S(1)}, u32[]{:S(2)}, u32[]{:S(2)}) collective-permute-start(bf16[8,3072]{1,0:T(8,128)(2,1)S(1)} %get-tuple-element.12), channel_id=1, source_target_pairs={{64,0},{65,1},{66,2},{67,3},{68,4},{69,5},{70,6},{71,7},{72,8},{73... | collective-permute-start | bytes 147464 | tf_op jit(solution)/shard_map/ppermute | solution.py:12
  439.6 38.7 %slice-start.4 = ((s8[6291456]{0:T(1024)(128)(4,1)}), s8[2097152]{0:T(1024)(128)(4,1)S(1)}, s32[]{:S(2)}) async-start(s8[6291456]{0:T(1024)(128)(4,1)} %bitcast.552), calls=%async_computation.18 | async-start | bytes 4194304
  439.6 29.2 %all-to-all-start.10 = ((bf16[64,3,3072]{2,1,0:T(4,128)(2,1)}), bf16[64,3,3072]{2,1,0:T(4,128)(2,1)}, u32[]{:S(2)}, u32[]{:S(2)}) async-start(bf16[64,3,3072]{2,1,0:T(4,128)(2,1)} %bitcast.567), calls=%async_computation.10 | async-start | bytes 3145728 | tf_op jit(solution)/shard_map/all_to_all | solution.py:41
  486.4 83.7 %all-to-all-start.11 = ((bf16[64,3,3072]{2,1,0:T(4,128)(2,1)}), bf16[64,3,3072]{2,1,0:T(4,128)(2,1)S(1)}, u32[]{:S(2)}, u32[]{:S(2)}) async-start(bf16[64,3,3072]{2,1,0:T(4,128)(2,1)} %reshape.604), calls=%async_computation.11 | async-start | bytes 3145728 | tf_op jit(solution)/shard_map/all_to_all | solution.py:48
  491.5 78.6 %all-reduce.3.cloned.1.call-start = ((), (), s32[]{:S(2)}) async-start(), calls=%async_computation.12 | async-start | bytes 196608 | tf_op jit(solution)/shard_map/psum | solution.py:222
  493.0 136.7 %all-reduce.5.cloned.1.call-start = ((), (), s32[]{:S(2)}) async-start(), calls=%async_computation.13 | async-start | bytes 196608 | tf_op jit(solution)/shard_map/psum | solution.py:222
  493.1 78.2 %copy-start.42 = (bf16[1,2,8,3072]{3,2,1,0:T(8,128)(2,1)}, bf16[1,2,8,3072]{3,2,1,0:T(8,128)(2,1)S(1)}, u32[]{:S(2)}) copy-start(bf16[1,2,8,3072]{3,2,1,0:T(8,128)(2,1)S(1)} %fusion.175) | copy-start | bytes 294916
  571.7 59.5 %copy-start.43 = (bf16[1,2,8,3072]{3,2,1,0:T(8,128)(2,1)}, bf16[1,2,8,3072]{3,2,1,0:T(8,128)(2,1)S(1)}, u32[]{:S(2)}) copy-start(bf16[1,2,8,3072]{3,2,1,0:T(8,128)(2,1)S(1)} %fusion.187) | copy-start | bytes 294916
  (81 other events, 475.7 us)
Sparse Core Ops, SparseCore 0:
  495.3 74.7 all-reduce.2
  572.4 57.1 all-reduce.4
